TPU v7x, 32 devices: a whole 2x2x4 slice. The times are simulated.
32 devices in a mesh: gx: 4 (over y, x), gy: 4 (over z), gz: 2 (over core).
Axes of the slice: x: 2, y: 2, z: 4, core: 2. Of those that a mesh axis runs over, the one named last changes fastest.
Arguments:
- state: float32 [16, 32, 64, 256], P('gx', 'gy', 'gz'), may hold values from -6 to 6
- convection: bfloat16 [16, 32, 64, 4096], P('gx', 'gy', 'gz'), may hold values from -0.375 to 0.375
- inverse_mass: bfloat16 [16, 32, 64, 4096], P('gx', 'gy', 'gz'), may hold values from -0.75 to 0.75
- face_coupling: bfloat16 [96, 64], replicated, may hold values from -0.3125 to 0.3125
- lower_bound: float32 [16, 32, 64, 256], P('gx', 'gy', 'gz'), may hold values from -3 to -1
- upper_bound: float32 [16, 32, 64, 256], P('gx', 'gy', 'gz'), may hold values from 1 to 3
- new_owner: int32 [32, 1024, 1], P(('gx', 'gy', 'gz')), may hold values from 0 to 31; in each aligned block of 1024 rows (0 to 1023, 1024 to 2047, ..., all dimensions but the last counted through in order) at most 64 rows name the same one
Outputs:
- handed: float32 [65536, 256], P(('gx', 'gy', 'gz'))
Inputs may be any that keep to these rules, and one draw needn't show every extreme that they name: `new_owner`: among the zones of one device no owner is named more than 64 times, a bound that some block reaches.
All inputs are finite; a program needn't handle non-finite values.
Results may differ from a plain program's by a relative error of at most 0.003.
Values may be sent and summed in bfloat16 or wider, within the bound.
A program may use at most 128 MiB of HBM per device.

v0:
```python
import jax
import jax.numpy as jnp
from jax import lax
from jax.sharding import PartitionSpec as P

COMP = 4
DOFS = 64
STEPS = 2


HIGH = lax.Precision.HIGHEST


def padded(cells, sides, width):
    for axis, dim in sides:
        count = lax.axis_size(axis)
        ends = count - 1
        head = lax.slice_in_dim(cells, 0, width, axis=dim)
        tail = lax.slice_in_dim(cells, cells.shape[dim] - width, cells.shape[dim], axis=dim)
        cells = jnp.concatenate(
            [
                lax.ppermute(tail, axis, [(i, (i + 1) % count) for i in range(ends)]),
                cells,
                lax.ppermute(head, axis, [((i + 1) % count, i) for i in range(ends)]),
            ],
            axis=dim,
        )
    return cells


def face_tables(face_coupling):
    columns = jnp.arange(COMP * DOFS, dtype=jnp.int32)
    component = columns // DOFS
    local = columns % DOFS
    first = local // 16
    second = local // 4 % 4
    third = local % 4
    coords = (first, second, third)
    rests = (4 * second + third, 4 * first + third, 4 * first + second)
    outputs = jnp.arange(COMP * 16, dtype=jnp.int32)
    out_comp = outputs // 16
    out_face = outputs % 16

    def select(direction, level):
        match = (
            (coords[direction] == level)[:, None]
            & (component[:, None] == out_comp[None, :])
            & (rests[direction][:, None] == out_face[None, :])
        )
        return match.astype(jnp.float32)

    identity = jnp.eye(COMP, dtype=jnp.float32)

    def couple(face):
        block = face_coupling[16 * face : 16 * face + 16].astype(jnp.float32)
        return jnp.einsum("cd,fi->cfdi", identity, block).reshape(COMP * 16, COMP * DOFS)

    picks = []
    whole = []
    spreads = []
    blank = jnp.zeros((COMP * 16, COMP * DOFS), jnp.float32)
    for direction in range(3):
        upper_pick = select(direction, 3)
        lower_pick = select(direction, 0)
        before = couple(2 * direction)
        after = couple(2 * direction + 1)
        whole.append(jnp.dot(upper_pick, before, precision=HIGH).astype(jnp.bfloat16))
        whole.append(jnp.dot(lower_pick, after, precision=HIGH).astype(jnp.bfloat16))
        picks.append(jnp.concatenate([upper_pick, lower_pick], axis=1).astype(jnp.bfloat16))
        spreads.append(
            (
                jnp.concatenate([before, blank], axis=0).astype(jnp.bfloat16),
                jnp.concatenate([blank, after], axis=0).astype(jnp.bfloat16),
            )
        )
    return (picks, whole, spreads)


def apply_table(piece, table):
    width = piece.shape[-1]
    return jnp.dot(piece.reshape(-1, width), table, preferred_element_type=jnp.float32)


def face_flux(work, tables):
    picks, whole, spreads = tables
    ex, ey, ez = (work.shape[0], work.shape[1], work.shape[2])
    rows = work.reshape(ex * ey * ez, COMP * DOFS)

    def payload(direction):
        return (
            jnp.dot(rows, picks[direction], preferred_element_type=jnp.float32)
            .astype(jnp.bfloat16)
            .reshape(ex, ey, ez, COMP * 32)
        )

    along_x = padded(payload(0), (("gx", 0),), 1)
    along_y = padded(payload(1), (("gy", 1),), 1)
    along_z = padded(payload(2), (("gz", 2),), 1)
    flux = apply_table(along_x[0:ex], spreads[0][0])
    flux = flux + apply_table(along_x[2 : ex + 2], spreads[0][1])
    flux = flux + apply_table(along_y[:, 0:ey], spreads[1][0])
    flux = flux + apply_table(along_y[:, 2 : ey + 2], spreads[1][1])
    flux = flux + apply_table(along_z[:, :, 0:ez], spreads[2][0])
    flux = flux + apply_table(along_z[:, :, 2 : ez + 2], spreads[2][1])
    return flux


def remap_step(state, convection, inverse_mass, tables, lower_bound, upper_bound):
    ex, ey, ez, width = state.shape
    zones = ex * ey * ez
    work = state.astype(jnp.bfloat16)
    flux = face_flux(work, tables)
    conv = convection.reshape(zones, DOFS, DOFS)
    pushed = jnp.einsum(
        "ecj,eij->eci", work.reshape(zones, COMP, DOFS), conv, preferred_element_type=jnp.float32
    )
    rhs = (pushed + flux.reshape(zones, COMP, DOFS)).astype(jnp.bfloat16)
    inverse = inverse_mass.reshape(zones, DOFS, DOFS)
    change = jnp.einsum("ecj,eij->eci", rhs, inverse, preferred_element_type=jnp.float32)
    moved = state + change.reshape(ex, ey, ez, width)
    return jnp.minimum(jnp.maximum(moved, lower_bound), upper_bound)


def shards(state, convection, inverse_mass, face_coupling, lower_bound, upper_bound, new_owner):
    tables = face_tables(face_coupling)
    for step in range(STEPS):
        state = remap_step(state, convection, inverse_mass, tables, lower_bound, upper_bound)
    ex, ey, ez, width = state.shape
    zones = ex * ey * ez
    devices = lax.axis_size(("gx", "gy", "gz"))
    capacity = max(2, 2 * zones // devices)
    rows = state.reshape(zones, width)
    owner = new_owner[0, :, 0]
    onehot = (owner[:, None] == jnp.arange(devices, dtype=jnp.int32)[None, :]).astype(jnp.bfloat16)
    positions = jnp.arange(zones, dtype=jnp.int32)
    lower_tri = (positions[:, None] >= positions[None, :]).astype(jnp.bfloat16)
    running = jnp.dot(lower_tri, onehot, preferred_element_type=jnp.float32)
    rank = jnp.sum(running * onehot.astype(jnp.float32), axis=1).astype(jnp.int32) - 1
    target = owner * capacity + rank
    outgoing = jnp.zeros((devices * capacity, width), jnp.float32).at[target].set(rows)
    arrived = lax.all_to_all(
        outgoing.reshape(devices, capacity, width),
        ("gx", "gy", "gz"),
        split_axis=0,
        concat_axis=0,
        tiled=True,
    )
    return arrived.reshape(devices * capacity, width)


def solution(mesh):
    in_specs = (
        P("gx", "gy", "gz", None),
        P("gx", "gy", "gz", None),
        P("gx", "gy", "gz", None),
        P(),
        P("gx", "gy", "gz", None),
        P("gx", "gy", "gz", None),
        P(("gx", "gy", "gz"), None, None),
    )
    out_specs = P(("gx", "gy", "gz"), None)
    return jax.shard_map(shards, mesh=mesh, in_specs=in_specs, out_specs=out_specs, check_vma=False)
```

profile of v0, /device:TPU:0, one launch (start us, length us, event | category | flops | bytes accessed | tf_op | source)
XLA Modules:
  0.0 217.9 jit_solution(18102308566268104938)
XLA Ops:
  0.1 1.3 convert_element_type.88
  1.6 0.3 fusion.10
  2.1 5.0 %collective-permute-start.2 = (bf16[4,1,32,128]{3,2,1,0:T(8,128)(2,1)S(1)}, bf16[4,1,32,128]{3,2,1,0:T(8,128)(2,1)S(1)}, u32[]{:S(2)}, u32[]{:S(2)}) collective-permute-start(bf16[4,1,32,128]{3,2,1,0:T(8,128)(2,1)S(1)} %get-tuple-element.23), channel_id=1, source_target_pairs={{0,2},{2,4},{4,6},{1,3},{3,5},{5,7},{8,10},{10,12},{12,14},{9,11},... | collective-permute-start | bytes 98312 | tf_op jit(solution)/shard_map/ppermute | solution.py:22
  7.1 1.3 collective-permute-start.3
  8.4 0.3 fusion.11
  8.9 1.5 collective-permute-start.4
  10.4 1.3 collective-permute-start.5
  11.7 0.3 fusion.9
  12.1 3.4 %collective-permute-start = (bf16[1,8,32,128]{3,2,1,0:T(8,128)(2,1)S(1)}, bf16[1,8,32,128]{3,2,1,0:T(8,128)(2,1)S(1)}, u32[]{:S(2)}, u32[]{:S(2)}) collective-permute-start(bf16[1,8,32,128]{3,2,1,0:T(8,128)(2,1)S(1)} %bitcast.119), channel_id=1, source_target_pairs={{0,8},{8,16},{16,24},{1,9},{9,17},{17,25},{2,10},{10,18},{18,26},{... | collective-permute-start | bytes 196616 | tf_op jit(solution)/shard_map/ppermute | solution.py:22
  16.2 0.6 fusion.13
  17.0 0.6 compare_select_fusion
  17.8 1.4 reshape.279
  20.0 23.6 %reshape.280 = bf16[1024,64,64]{2,1,0:T(8,128)(2,1)} reshape(bf16[4,8,32,4096]{3,2,1,0:T(8,128)(2,1)} %param.8) | data formatting | bytes 16777216 | tf_op jit(solution)/shard_map/reshape | solution.py:113
  43.6 23.6 %reshape.298 = bf16[1024,64,64]{2,1,0:T(8,128)(2,1)} reshape(bf16[4,8,32,4096]{3,2,1,0:T(8,128)(2,1)} %param.9) | data formatting | bytes 16777216 | tf_op jit(solution)/shard_map/reshape | solution.py:118
  67.2 1.5 collective-permute-start.1
  68.9 0.3 fusion.22
  69.2 0.3 fusion.26
  69.6 0.3 fusion.30
  70.0 0.3 fusion.34
  70.3 3.6 %collective-permute-done.1 = bf16[1,8,32,128]{3,2,1,0:T(8,128)(2,1)S(1)} collective-permute-done((bf16[1,8,32,128]{3,2,1,0:T(8,128)(2,1)S(1)}, bf16[1,8,32,128]{3,2,1,0:T(8,128)(2,1)S(1)}, u32[]{:S(2)}, u32[]{:S(2)}) %collective-permute-start.1) | collective-permute-done | bytes 65568 | tf_op jit(solution)/shard_map/ppermute | solution.py:24
  74.0 0.3 fusion.38
  74.3 0.4 fusion.8
  74.8 0.9 copy.55
  75.7 22.9 %fusion.16 = f32[1024,4,64]{2,1,0:T(4,128)} fusion(bf16[1024,64,64]{2,1,0:T(8,128)(2,1)} %reshape.298, f32[1024,4,64]{2,1,0:T(4,128)S(1)} %copy.55, bf16[1024,4,64]{2,1,0:T(4,128)(2,1)} %reshape.279, bf16[1024,64,64]{2,1,0:T(8,128)(2,1)} %reshape.280), kind=kOutput, calls=%fused_computation.30 | convolution fusion | flops 67633152 | bytes 19398656 | tf_op jit(solution)/shard_map/ecj,eij->eci/dot_general | solution.py:119
  98.5 2.6 %reshape.299 = f32[4,8,32,256]{3,2,1,0:T(8,128)S(1)} reshape(f32[1024,4,64]{2,1,0:T(4,128)} %fusion.16) | data formatting | bytes 2097152 | tf_op jit(solution)/shard_map/reshape | solution.py:120
  101.1 1.9 fusion.18
  103.6 0.3 convolution_convert_fusion
  103.9 1.4 reshape.300
  105.3 4.3 %collective-permute-start.6 = (bf16[1,8,32,128]{3,2,1,0:T(8,128)(2,1)S(1)}, bf16[1,8,32,128]{3,2,1,0:T(8,128)(2,1)S(1)}, u32[]{:S(2)}, u32[]{:S(2)}) collective-permute-start(bf16[1,8,32,128]{3,2,1,0:T(8,128)(2,1)S(1)} %bitcast.122), channel_id=1, source_target_pairs={{0,8},{8,16},{16,24},{1,9},{9,17},{17,25},{2,10},{10,18},{18,26},{... | collective-permute-start | bytes 196616 | tf_op jit(solution)/shard_map/ppermute | solution.py:22
  109.6 1.3 collective-permute-start.7
  111.0 1.6 collective-permute-start.10
  112.6 1.3 collective-permute-start.11
  113.9 4.4 %collective-permute-start.8 = (bf16[4,1,32,128]{3,2,1,0:T(8,128)(2,1)S(1)}, bf16[4,1,32,128]{3,2,1,0:T(8,128)(2,1)S(1)}, u32[]{:S(2)}, u32[]{:S(2)}) collective-permute-start(bf16[4,1,32,128]{3,2,1,0:T(8,128)(2,1)S(1)} %get-tuple-element.11), channel_id=1, source_target_pairs={{0,2},{2,4},{4,6},{1,3},{3,5},{5,7},{8,10},{10,12},{12,14},{9,11},... | collective-permute-start | bytes 98312 | tf_op jit(solution)/shard_map/ppermute | solution.py:22
  118.3 1.5 collective-permute-start.9
  120.0 1.1 fusion.24
  121.1 0.3 fusion.20
  121.5 2.8 %collective-permute-done.9 = bf16[4,1,32,128]{3,2,1,0:T(8,128)(2,1)S(1)} collective-permute-done((bf16[4,1,32,128]{3,2,1,0:T(8,128)(2,1)S(1)}, bf16[4,1,32,128]{3,2,1,0:T(8,128)(2,1)S(1)}, u32[]{:S(2)}, u32[]{:S(2)}) %collective-permute-start.9) | collective-permute-done | bytes 32800 | tf_op jit(solution)/shard_map/ppermute | solution.py:24
  124.4 0.3 fusion.32
  124.7 0.3 fusion.28
  125.1 0.3 fusion.36
  125.5 0.4 fusion.4
  125.9 1.7 copy.56
  127.7 23.1 %fusion.17 = f32[1024,4,64]{2,1,0:T(4,128)} fusion(bf16[1024,64,64]{2,1,0:T(8,128)(2,1)} %reshape.298, f32[1024,4,64]{2,1,0:T(4,128)} %copy.56, bf16[1024,4,64]{2,1,0:T(4,128)(2,1)} %reshape.300, bf16[1024,64,64]{2,1,0:T(8,128)(2,1)} %reshape.280), kind=kOutput, calls=%fused_computation.31 | convolution fusion | flops 67633152 | bytes 19398656 | tf_op jit(solution)/shard_map/ecj,eij->eci/dot_general | solution.py:119
  150.7 2.5 %reshape.312 = f32[4,8,32,256]{3,2,1,0:T(8,128)S(1)} reshape(f32[1024,4,64]{2,1,0:T(4,128)} %fusion.17) | data formatting | bytes 2097152 | tf_op jit(solution)/shard_map/reshape | solution.py:120
  153.2 3.1 %maximum_minimum_fusion = f32[4,8,32,256]{3,2,1,0:T(8,128)} fusion(f32[4,8,32,256]{3,2,1,0:T(8,128)} %param.12, f32[4,8,32,256]{3,2,1,0:T(8,128)} %param.11, f32[4,8,32,256]{3,2,1,0:T(8,128)S(1)} %reshape.312, f32[4,8,32,256]{3,2,1,0:T(8,128)S(1)} %copy-done, f32[4,8,32,256]{3,2,1,0:T(8,128)S(1)} %reshape.299), kind=kLoop, calls=%fused_computation.26 | loop fusion | flops 1572864 | bytes 6291456 | tf_op jit(solution)/shard_map/min | solution.py:121
  156.3 5.8 %scatter_custom_fusion = f32[2048,256]{1,0:T(8,128)S(1)} fusion(s32[1024]{0:T(1024)} %bitcast.125, f32[1024,256]{1,0:T(8,128)} %bitcast.118, f32[]{:T(128)} %constant.91.clone.1), kind=kCustom, calls=%fused_computation.28 | custom fusion | bytes 2097664 | tf_op jit(solution)/shard_map/scatter | solution.py:140
  162.1 54.5 %all_to_all.5 = f32[32,64,256]{2,1,0:T(8,128)S(1)} all-to-all(f32[32,64,256]{2,1,0:T(8,128)S(1)} %bitcast.92), channel_id=1, replica_groups=mesh['gx'=4,'gy'=4,'gz'=2] {'gx','gy','gz'}, dimensions={0} | all-to-all | bytes 4194304 | tf_op jit(solution)/shard_map/all_to_all | solution.py:141
  216.6 1.3 copy.82
  (74 shorter events, 3.8 us)
Async XLA Ops:
  1.4 14.1 %copy-start.1 = (bf16[96,64]{0,1:T(8,128)(2,1)S(1)}, bf16[96,64]{0,1:T(8,128)(2,1)}, u32[]{:S(2)}) copy-start(bf16[96,64]{0,1:T(8,128)(2,1)} %param.10) | copy-start | bytes 36868
  1.6 6.8 %copy-start.5 = (pred[256,64]{0,1:T(32,128)(4,1)}, pred[256,64]{0,1:T(32,128)(4,1)S(1)}, u32[]{:S(2)}) copy-start(pred[256,64]{0,1:T(32,128)(4,1)S(1)} %get-tuple-element.48) | copy-start | bytes 49156
  1.6 14.6 %copy-start.7 = (s32[1,1024,1]{1,2,0:T(1,128)S(1)}, s32[1,1024,1]{1,2,0:T(1,128)}, u32[]{:S(2)}) copy-start(s32[1,1024,1]{1,2,0:T(1,128)} %param.13) | copy-start | bytes 12292
  2.1 67.5 %collective-permute-start.2 = (bf16[4,1,32,128]{3,2,1,0:T(8,128)(2,1)S(1)}, bf16[4,1,32,128]{3,2,1,0:T(8,128)(2,1)S(1)}, u32[]{:S(2)}, u32[]{:S(2)}) collective-permute-start(bf16[4,1,32,128]{3,2,1,0:T(8,128)(2,1)S(1)} %get-tuple-element.23), channel_id=1, source_target_pairs={{0,2},{2,4},{4,6},{1,3},{3,5},{5,7},{8,10},{10,12},{12,14},{9,11},... | collective-permute-start | bytes 98312 | tf_op jit(solution)/shard_map/ppermute | solution.py:22
  7.1 62.5 %collective-permute-start.3 = (bf16[4,1,32,128]{3,2,1,0:T(8,128)(2,1)S(1)}, bf16[4,1,32,128]{3,2,1,0:T(8,128)(2,1)S(1)}, u32[]{:S(2)}, u32[]{:S(2)}) collective-permute-start(bf16[4,1,32,128]{3,2,1,0:T(8,128)(2,1)S(1)} %get-tuple-element.24), channel_id=1, source_target_pairs={{2,0},{4,2},{6,4},{3,1},{5,3},{7,5},{10,8},{12,10},{14,12},{11,9},... | collective-permute-start | bytes 98312 | tf_op jit(solution)/shard_map/ppermute | solution.py:24
  8.9 58.3 %collective-permute-start.4 = (bf16[4,8,1,128]{3,2,1,0:T(2,128)(2,1)S(1)}, bf16[4,8,1,128]{3,2,1,0:T(2,128)(2,1)S(1)}, u32[]{:S(2)}, u32[]{:S(2)}) collective-permute-start(bf16[4,8,1,128]{3,2,1,0:T(2,128)(2,1)S(1)} %get-tuple-element.27), channel_id=1, source_target_pairs={{0,1},{2,3},{4,5},{6,7},{8,9},{10,11},{12,13},{14,15},{16,17},{18,... | collective-permute-start | bytes 24584 | tf_op jit(solution)/shard_map/ppermute | solution.py:22
  10.4 58.3 %collective-permute-start.5 = (bf16[4,8,1,128]{3,2,1,0:T(2,128)(2,1)S(1)}, bf16[4,8,1,128]{3,2,1,0:T(2,128)(2,1)S(1)}, u32[]{:S(2)}, u32[]{:S(2)}) collective-permute-start(bf16[4,8,1,128]{3,2,1,0:T(2,128)(2,1)S(1)} %get-tuple-element.28), channel_id=1, source_target_pairs={{1,0},{3,2},{5,4},{7,6},{9,8},{11,10},{13,12},{15,14},{17,16},{19,... | collective-permute-start | bytes 24584 | tf_op jit(solution)/shard_map/ppermute | solution.py:24
  12.1 58.2 %collective-permute-start = (bf16[1,8,32,128]{3,2,1,0:T(8,128)(2,1)S(1)}, bf16[1,8,32,128]{3,2,1,0:T(8,128)(2,1)S(1)}, u32[]{:S(2)}, u32[]{:S(2)}) collective-permute-start(bf16[1,8,32,128]{3,2,1,0:T(8,128)(2,1)S(1)} %bitcast.119), channel_id=1, source_target_pairs={{0,8},{8,16},{16,24},{1,9},{9,17},{17,25},{2,10},{10,18},{18,26},{... | collective-permute-start | bytes 196616 | tf_op jit(solution)/shard_map/ppermute | solution.py:22
  19.5 49.3 %copy-start.2 = (bf16[64,256]{1,0:T(8,128)(2,1)}, bf16[64,256]{1,0:T(8,128)(2,1)S(1)}, u32[]{:S(2)}) copy-start(bf16[64,256]{1,0:T(8,128)(2,1)S(1)} %reshape.296) | copy-start | bytes 98308
  19.7 49.6 %copy-start.4 = (bf16[64,256]{1,0:T(8,128)(2,1)}, bf16[64,256]{1,0:T(8,128)(2,1)S(1)}, u32[]{:S(2)}) copy-start(bf16[64,256]{1,0:T(8,128)(2,1)S(1)} %reshape.294) | copy-start | bytes 98308
  67.2 6.7 %collective-permute-start.1 = (bf16[1,8,32,128]{3,2,1,0:T(8,128)(2,1)S(1)}, bf16[1,8,32,128]{3,2,1,0:T(8,128)(2,1)S(1)}, u32[]{:S(2)}, u32[]{:S(2)}) collective-permute-start(bf16[1,8,32,128]{3,2,1,0:T(8,128)(2,1)S(1)} %bitcast.120), channel_id=1, source_target_pairs={{8,0},{16,8},{24,16},{9,1},{17,9},{25,17},{10,2},{18,10},{26,18},{... | collective-permute-start | bytes 196616 | tf_op jit(solution)/shard_map/ppermute | solution.py:24
  98.5 2.6 %copy-start = (f32[4,8,32,256]{3,2,1,0:T(8,128)S(1)}, f32[4,8,32,256]{3,2,1,0:T(8,128)}, u32[]{:S(2)}) copy-start(f32[4,8,32,256]{3,2,1,0:T(8,128)} %param.7) | copy-start | bytes 3145732
  101.1 2.5 %copy-start.6 = (pred[256,64]{0,1:T(32,128)(4,1)S(1)}, pred[256,64]{0,1:T(32,128)(4,1)}, u32[]{:S(2)}) copy-start(pred[256,64]{0,1:T(32,128)(4,1)} %copy-done.5) | copy-start | bytes 49156
  105.3 15.8 %copy-start.3 = (bf16[64,256]{1,0:T(8,128)(2,1)S(1)}, bf16[64,256]{1,0:T(8,128)(2,1)}, u32[]{:S(2)}) copy-start(bf16[64,256]{1,0:T(8,128)(2,1)} %copy-done.2) | copy-start | bytes 98308
  105.3 19.7 %collective-permute-start.6 = (bf16[1,8,32,128]{3,2,1,0:T(8,128)(2,1)S(1)}, bf16[1,8,32,128]{3,2,1,0:T(8,128)(2,1)S(1)}, u32[]{:S(2)}, u32[]{:S(2)}) collective-permute-start(bf16[1,8,32,128]{3,2,1,0:T(8,128)(2,1)S(1)} %bitcast.122), channel_id=1, source_target_pairs={{0,8},{8,16},{16,24},{1,9},{9,17},{17,25},{2,10},{10,18},{18,26},{... | collective-permute-start | bytes 196616 | tf_op jit(solution)/shard_map/ppermute | solution.py:22
  109.6 15.4 %collective-permute-start.7 = (bf16[1,8,32,128]{3,2,1,0:T(8,128)(2,1)S(1)}, bf16[1,8,32,128]{3,2,1,0:T(8,128)(2,1)S(1)}, u32[]{:S(2)}, u32[]{:S(2)}) collective-permute-start(bf16[1,8,32,128]{3,2,1,0:T(8,128)(2,1)S(1)} %bitcast.121), channel_id=1, source_target_pairs={{8,0},{16,8},{24,16},{9,1},{17,9},{25,17},{10,2},{18,10},{26,18},{... | collective-permute-start | bytes 196616 | tf_op jit(solution)/shard_map/ppermute | solution.py:24
  111.0 7.3 %collective-permute-start.10 = (bf16[4,8,1,128]{3,2,1,0:T(2,128)(2,1)S(1)}, bf16[4,8,1,128]{3,2,1,0:T(2,128)(2,1)S(1)}, u32[]{:S(2)}, u32[]{:S(2)}) collective-permute-start(bf16[4,8,1,128]{3,2,1,0:T(2,128)(2,1)S(1)} %get-tuple-element.15), channel_id=1, source_target_pairs={{0,1},{2,3},{4,5},{6,7},{8,9},{10,11},{12,13},{14,15},{16,17},{18,... | collective-permute-start | bytes 24584 | tf_op jit(solution)/shard_map/ppermute | solution.py:22
  112.6 7.2 %collective-permute-start.11 = (bf16[4,8,1,128]{3,2,1,0:T(2,128)(2,1)S(1)}, bf16[4,8,1,128]{3,2,1,0:T(2,128)(2,1)S(1)}, u32[]{:S(2)}, u32[]{:S(2)}) collective-permute-start(bf16[4,8,1,128]{3,2,1,0:T(2,128)(2,1)S(1)} %get-tuple-element.16), channel_id=1, source_target_pairs={{1,0},{3,2},{5,4},{7,6},{9,8},{11,10},{13,12},{15,14},{17,16},{19,... | collective-permute-start | bytes 24584 | tf_op jit(solution)/shard_map/ppermute | solution.py:24
  113.9 7.6 %collective-permute-start.8 = (bf16[4,1,32,128]{3,2,1,0:T(8,128)(2,1)S(1)}, bf16[4,1,32,128]{3,2,1,0:T(8,128)(2,1)S(1)}, u32[]{:S(2)}, u32[]{:S(2)}) collective-permute-start(bf16[4,1,32,128]{3,2,1,0:T(8,128)(2,1)S(1)} %get-tuple-element.11), channel_id=1, source_target_pairs={{0,2},{2,4},{4,6},{1,3},{3,5},{5,7},{8,10},{10,12},{12,14},{9,11},... | collective-permute-start | bytes 98312 | tf_op jit(solution)/shard_map/ppermute | solution.py:22
  118.3 6.0 %collective-permute-start.9 = (bf16[4,1,32,128]{3,2,1,0:T(8,128)(2,1)S(1)}, bf16[4,1,32,128]{3,2,1,0:T(8,128)(2,1)S(1)}, u32[]{:S(2)}, u32[]{:S(2)}) collective-permute-start(bf16[4,1,32,128]{3,2,1,0:T(8,128)(2,1)S(1)} %get-tuple-element.12), channel_id=1, source_target_pairs={{2,0},{4,2},{6,4},{3,1},{5,3},{7,5},{10,8},{12,10},{14,12},{11,9},... | collective-permute-start | bytes 98312 | tf_op jit(solution)/shard_map/ppermute | solution.py:24
where the time goes:
time: 220 us; the launch traced here: 218 us
  local copies, waits for them, and re-layouts  66.9 us (30%)
  blocking collectives  54.5 us (25%)
  matrix products  53.3 us (24%)
  starting transfers between devices  28.3 us (13%)
  other arithmetic  7.98 us (4%)
  waiting for transfers between devices  6.46 us (3%)
    all_to_all x1, blocking collectives, shards(): lax.all_to_all(outgoing.reshape(devices, capacity, width), ('gx', 'gy', '...  54.5 us
    dot_general x2, matrix products, remap_step(): jnp.einsum('ecj,eij->eci', rhs, inverse, preferred_element_type=jnp.float32)  45.9 us
    reshape x1, local copies, waits for them, and re-layouts, remap_step(): conv = convection.reshape(zones, DOFS, DOFS)  23.6 us
    reshape x1, local copies, waits for them, and re-layouts, remap_step(): inverse = inverse_mass.reshape(zones, DOFS, DOFS)  23.6 us
    ppermute x6, starting transfers between devices, padded(): lax.ppermute(tail, axis, [(i, (i + 1) % count) for i in range(ends)])  20.1 us
    ppermute x6, starting transfers between devices, padded(): lax.ppermute(head, axis, [((i + 1) % count, i) for i in range(ends)])  8.14 us
    ppermute x6, waiting for transfers between devices, padded(): lax.ppermute(head, axis, [((i + 1) % count, i) for i in range(ends)])  6.45 us
    scatter x1, local copies, waits for them, and re-layouts, shards(): jnp.zeros((devices * capacity, width), jnp.float32).at[target].set(rows)  5.78 us
  transfers between devices with their start and end apart: 12, of which 2 were waited for; matrix products, arithmetic and copies ran while one was open for 26% of the time, Pallas kernels for 0%

commit v1 on v0

v1 whole, which is shorter than its diff:
```python
import functools
import jax
import jax.numpy as jnp
from jax import lax
from jax.experimental import pallas as pl
from jax.experimental.pallas import tpu as pltpu
from jax.sharding import PartitionSpec as P

COMP = 4
DOFS = 64
WIDTH = COMP * DOFS
STEPS = 2
LANES = 256
WIDE = (True, True)
MESH = pl.DeviceIdType.MESH
BF = jnp.bfloat16
F32 = jnp.float32
NT = (((1,), (1,)), ((), ()))


def face_tables(face_coupling):
    columns = jnp.arange(WIDTH, dtype=jnp.int32)
    component = columns // DOFS
    local = columns % DOFS
    coords = (local // 16, local // 4 % 4, local % 4)
    rests = (4 * coords[1] + coords[2], 4 * coords[0] + coords[2], 4 * coords[0] + coords[1])
    outputs = jnp.arange(COMP * 16, dtype=jnp.int32)
    picks = []
    couples = []
    identity = jnp.eye(COMP, dtype=BF)
    for direction in range(3):
        for side, level in ((0, 3), (1, 0)):
            match = (
                (coords[direction] == level)[None, :]
                & (component[None, :] == (outputs // 16)[:, None])
                & (rests[direction][None, :] == (outputs % 16)[:, None])
            )
            picks.append(match.astype(BF))
            face = 2 * direction + side
            block = face_coupling[16 * face : 16 * face + 16]
            couples.append(
                (identity[:, None, :, None] * block.T[None, :, None, :]).reshape(WIDTH, COMP * 16)
            )
    return jnp.concatenate(picks, axis=0), jnp.concatenate(couples, axis=1)


def kernel(
    dims, cap,
    state_ref, lower_ref, upper_ref, slot_ref, pick_ref, couple_ref, eye_ref, gather_ref,
    conv_hbm, inv_hbm, out_ref,
    conv_raw, inv_raw, conv_t, inv_t, state_t, lower_t, upper_t, work, rhs, partial,
    faces, landed, load_sem, send_sem, recv_sem,
):
    zones = state_ref.shape[0]
    blocks = zones // LANES
    axes = ("gx", "gy", "gz")
    counts = [lax.axis_size(a) for a in axes]
    place = [lax.axis_index(a) for a in axes]
    strides = (dims[1] * dims[2], dims[2], 1)

    def loads(block, inverse):
        part = pl.ds(block * LANES, LANES)
        if inverse:
            return pltpu.make_async_copy(inv_hbm.at[part], inv_raw.at[part], load_sem.at[blocks + block])
        return pltpu.make_async_copy(conv_hbm.at[part], conv_raw.at[part], load_sem.at[block])

    for block in range(blocks):
        loads(block, False).start()
    for block in range(blocks):
        loads(block, True).start()

    landed[...] = jnp.zeros_like(landed)
    barrier = pltpu.get_barrier_semaphore()
    ups = [place[d] < counts[d] - 1 for d in range(3)]
    downs = [place[d] > 0 for d in range(3)]
    for d in range(3):
        @pl.when(ups[d])
        def _(d=d):
            pl.semaphore_signal(barrier, 1, device_id={axes[d]: place[d] + 1}, device_id_type=MESH)

        @pl.when(downs[d])
        def _(d=d):
            pl.semaphore_signal(barrier, 1, device_id={axes[d]: place[d] - 1}, device_id_type=MESH)
    pl.semaphore_wait(barrier, sum(flag.astype(jnp.int32) for flag in ups + downs))

    for block in range(blocks):
        part = pl.ds(block * LANES, LANES)
        state_t[:, part] = state_ref[part, :].T
        lower_t[:, part] = lower_ref[part, :].T
        upper_t[:, part] = upper_ref[part, :].T

    rows = COMP * 16

    def exchange(step, d, side):
        row = pl.ds((2 * d + side) * rows, rows)
        if d == 0:
            near = zones - strides[0] if side == 0 else 0
            lane = pl.ds(near, strides[0])
        else:
            lane = pl.ds(0, zones)
        return pltpu.make_async_remote_copy(
            src_ref=faces.at[step, row, lane],
            dst_ref=landed.at[step, row, lane],
            send_sem=send_sem.at[step, 2 * d + side],
            recv_sem=recv_sem.at[step, 2 * d + side],
            device_id={axes[d]: place[d] + 1 if side == 0 else place[d] - 1},
            device_id_type=MESH,
        )

    def transposed(raw, target, block):
        @pl.loop(0, DOFS * DOFS // LANES)
        def _(chunk):
            col = pl.ds(pl.multiple_of(chunk * LANES, LANES), LANES)
            part = pl.ds(block * LANES, LANES)
            target[col, part] = lax.dot_general(
                eye_ref[...], raw[part, col], NT, preferred_element_type=F32
            ).astype(BF)

    def apply(matrix, vector, block, wide):
        part = pl.ds(block * LANES, LANES)

        @pl.loop(0, DOFS // 4)
        def _(group):
            for half in range(LANES // 128):
                lane = pl.ds(block * LANES + half * 128, 128)
                small = pl.ds(half * 128, 128)
                vecs = [
                    [vector[c * DOFS + 16 * b : c * DOFS + 16 * b + 16, lane] for b in range(4)]
                    for c in range(COMP)
                ]
                if wide:
                    vecs = [[piece.astype(F32) for piece in v] for v in vecs]
                for i in range(4):
                    base = pl.multiple_of(group * 256 + i * 64, 64)
                    m = [matrix[pl.ds(base + 16 * b, 16), lane] for b in range(4)]
                    if wide:
                        m = [piece.astype(F32) for piece in m]
                    for c in range(COMP):
                        v = vecs[c]
                        total = (m[0] * v[0] + m[1] * v[1]) + (m[2] * v[2] + m[3] * v[3])
                        slot = pl.ds(pl.multiple_of(group * 64 + i * 16, 16), 16)
                        partial[c, slot, small] = total.astype(BF)

        return [
            jnp.dot(gather_ref[...], partial[c], preferred_element_type=F32) for c in range(COMP)
        ]

    lane_id = lax.broadcasted_iota(jnp.int32, (rows, zones), 1)

    for step in range(STEPS):
        work[...] = state_t[...].astype(BF)
        faces[step] = jnp.dot(pick_ref[...], work[...], preferred_element_type=F32).astype(BF)
        for d in range(3):
            @pl.when(ups[d])
            def _(d=d):
                exchange(step, d, 0).start()

            @pl.when(downs[d])
            def _(d=d):
                exchange(step, d, 1).start()
        pushed = []
        for block in range(blocks):
            part = pl.ds(block * LANES, LANES)
            if step == 0:
                loads(block, False).wait()
                transposed(conv_raw, conv_t, block)
            for c, value in enumerate(apply(conv_t, work, block, WIDE[0])):
                rhs[c * DOFS : (c + 1) * DOFS, part] = value
        flux = None
        for d in range(3):
            @pl.when(downs[d])
            def _(d=d):
                exchange(step, d, 0).wait_recv()

            @pl.when(ups[d])
            def _(d=d):
                exchange(step, d, 1).wait_recv()
        for d in range(3):
            s = strides[d]
            n = dims[d]
            index = lane_id // s % n
            far = (n - 1) * s
            for side in range(2):
                row = pl.ds((2 * d + side) * rows, rows)
                mine = faces[step, row, :].astype(F32)
                other = landed[step, row, :].astype(F32)
                if side == 0:
                    inner = pltpu.roll(mine, s, 1)
                    outer = pltpu.roll(other, zones - far, 1)
                    value = jnp.where(index == 0, outer, inner)
                else:
                    inner = pltpu.roll(mine, zones - s, 1)
                    outer = pltpu.roll(other, far, 1)
                    value = jnp.where(index == n - 1, outer, inner)
                term = jnp.dot(
                    couple_ref[:, (2 * d + side) * rows : (2 * d + side + 1) * rows],
                    value.astype(BF),
                    preferred_element_type=F32,
                )
                flux = term if flux is None else flux + term
        work[...] = (rhs[...] + flux).astype(BF)
        for block in range(blocks):
            part = pl.ds(block * LANES, LANES)
            if step == 0:
                loads(block, True).wait()
                transposed(inv_raw, inv_t, block)
            for c, value in enumerate(apply(inv_t, work, block, WIDE[1])):
                row = slice(c * DOFS, (c + 1) * DOFS)
                moved = state_t[row, part] + value
                state_t[row, part] = jnp.minimum(
                    jnp.maximum(moved, lower_t[row, part]), upper_t[row, part]
                )
        for d in range(3):
            @pl.when(ups[d])
            def _(d=d):
                exchange(step, d, 0).wait_send()

            @pl.when(downs[d])
            def _(d=d):
                exchange(step, d, 1).wait_send()

    work[...] = state_t[...].astype(BF)
    slots = jnp.broadcast_to(slot_ref[...], (LANES, zones))
    level = lax.broadcasted_iota(jnp.int32, (LANES, zones), 0)

    @pl.loop(0, out_ref.shape[0] // LANES)
    def _(group):
        start = pl.multiple_of(group * LANES, LANES)
        onehot = jnp.where(slots == level + start, 1.0, 0.0).astype(BF)
        out_ref[pl.ds(start, LANES), :] = lax.dot_general(
            onehot, work[...], NT, preferred_element_type=F32
        ).astype(BF)


def shards(state, convection, inverse_mass, face_coupling, lower_bound, upper_bound, new_owner):
    ex, ey, ez, width = state.shape
    zones = ex * ey * ez
    devices = lax.axis_size(("gx", "gy", "gz"))
    capacity = max(2, 2 * zones // devices)
    pick, couple = face_tables(face_coupling)
    owner = new_owner[0, :, 0]
    onehot = (owner[:, None] == jnp.arange(devices, dtype=jnp.int32)[None, :]).astype(BF)
    positions = jnp.arange(zones, dtype=jnp.int32)
    lower_tri = (positions[:, None] >= positions[None, :]).astype(BF)
    running = jnp.dot(lower_tri, onehot, preferred_element_type=F32)
    rank = jnp.sum(running * onehot.astype(F32), axis=1).astype(jnp.int32) - 1
    slot = (owner * capacity + rank).reshape(1, zones)
    eye = jnp.eye(LANES, dtype=BF)
    gather = (
        jnp.arange(DOFS)[:, None] == (jnp.arange(DOFS * 16) // 16)[None, :]
    ).astype(BF)
    total = devices * capacity
    vmem = pl.BlockSpec(memory_space=pltpu.VMEM)
    hbm = pl.BlockSpec(memory_space=pl.ANY)
    blocks = zones // LANES
    entries = DOFS * DOFS
    outgoing = pl.pallas_call(
        functools.partial(kernel, (ex, ey, ez), capacity),
        out_shape=jax.ShapeDtypeStruct((total, width), BF),
        in_specs=[vmem] * 8 + [hbm] * 2,
        out_specs=vmem,
        scratch_shapes=[
            pltpu.VMEM((zones, entries), BF),
            pltpu.VMEM((zones, entries), BF),
            pltpu.VMEM((entries, zones), BF),
            pltpu.VMEM((entries, zones), BF),
            pltpu.VMEM((width, zones), F32),
            pltpu.VMEM((width, zones), F32),
            pltpu.VMEM((width, zones), F32),
            pltpu.VMEM((width, zones), BF),
            pltpu.VMEM((width, zones), F32),
            pltpu.VMEM((COMP, DOFS * 16, LANES), BF),
            pltpu.VMEM((STEPS, 6 * COMP * 16, zones), BF),
            pltpu.VMEM((STEPS, 6 * COMP * 16, zones), BF),
            pltpu.SemaphoreType.DMA((2 * blocks,)),
            pltpu.SemaphoreType.DMA((STEPS, 6)),
            pltpu.SemaphoreType.DMA((STEPS, 6)),
        ],
        compiler_params=pltpu.CompilerParams(
            collective_id=0, has_side_effects=True, vmem_limit_bytes=60 * 1024 * 1024
        ),
    )(
        state.reshape(zones, width), lower_bound.reshape(zones, width),
        upper_bound.reshape(zones, width), slot, pick, couple, eye, gather,
        convection.reshape(zones, entries), inverse_mass.reshape(zones, entries),
    )
    arrived = lax.all_to_all(
        outgoing.reshape(devices, capacity, width),
        ("gx", "gy", "gz"),
        split_axis=0,
        concat_axis=0,
        tiled=True,
    )
    return arrived.reshape(total, width).astype(F32)


def solution(mesh):
    in_specs = (
        P("gx", "gy", "gz", None),
        P("gx", "gy", "gz", None),
        P("gx", "gy", "gz", None),
        P(),
        P("gx", "gy", "gz", None),
        P("gx", "gy", "gz", None),
        P(("gx", "gy", "gz"), None, None),
    )
    out_specs = P(("gx", "gy", "gz"), None)
    return jax.shard_map(shards, mesh=mesh, in_specs=in_specs, out_specs=out_specs, check_vma=False)
```

time: 220 us -> 121 us (0.55)
  Pallas kernels: 0 us -> 77.5 us
  local copies, waits for them, and re-layouts: 66.9 us -> 3.74 us
  matrix products: 53.3 us -> 1.3 us
  starting transfers between devices: 28.3 us -> 0 us
  blocking collectives: 54.5 us -> 32.3 us
  waiting for transfers between devices: 6.46 us -> 0 us
    pallas_call x0 -> x1, Pallas kernels: none -> 77.5 us  [shards(): pl.pallas_call(functools.partial(kernel, (ex, ey, ez), capacity), out_sha...]
    reshape x14 -> x0, local copies, waits for them, and re-layouts: 58.3 us -> none  [the longest x1 23.6 us: remap_step(): conv = convection.reshape(zones, DOFS, DOFS)]
    dot_general x21 -> x1, matrix products: 53.3 us -> 1.3 us  [shards(): running = jnp.dot(lower_tri, onehot, preferred_element_type=F32)]
    ppermute x12 -> x0, starting transfers between devices: 28.3 us -> none  [the longest x6 20.1 us: padded(): lax.ppermute(tail, axis, [(i, (i + 1) % count) for i in range(ends)])]
    all_to_all x1, blocking collectives: 54.5 us -> 32.3 us  [shards(): lax.all_to_all(outgoing.reshape(devices, capacity, width), ('gx', 'gy', '...]
    ppermute x12 -> x0, waiting for transfers between devices: 6.46 us -> none  [the longest x6 6.45 us: padded(): lax.ppermute(head, axis, [((i + 1) % count, i) for i in range(ends)])]
    scatter x1 -> x0, local copies, waits for them, and re-layouts: 5.78 us -> none  [shards(): jnp.zeros((devices * capacity, width), jnp.float32).at[target].set(rows)]
    min x1 -> x0, other arithmetic: 3.07 us -> none  [remap_step(): return jnp.minimum(jnp.maximum(moved, lower_bound), upper_bound)]
  transfers between devices with their start and end apart: 12 -> 0, of which waited for: 2 -> 0; matrix products, arithmetic and copies ran while one was open for 26% -> 0% of each run, Pallas kernels for 0% -> 0%
where the time goes in v1:
time: 121 us
  Pallas kernels  77.5 us (64%)
  blocking collectives  32.3 us (27%)
  other arithmetic  5.81 us (5%)
  local copies, waits for them, and re-layouts  3.74 us (3%)
  matrix products  1.3 us (1%)
    pallas_call x1, Pallas kernels, shards(): pl.pallas_call(functools.partial(kernel, (ex, ey, ez), capacity), out_sha...  77.5 us
    all_to_all x1, blocking collectives, shards(): lax.all_to_all(outgoing.reshape(devices, capacity, width), ('gx', 'gy', '...  32.3 us

profile of v1, /device:TPU:0, one launch (start us, length us, event | category | flops | bytes accessed | tf_op | source)
XLA Modules:
  0.0 120.8 jit_solution(4884721433467447270)
XLA Ops:
  0.2 0.7 fusion.3.eye_ref
  0.8 1.3 %fusion.2 = f32[1024]{0:T(1024)S(1)} fusion(s32[1024]{0:T(1024)} %bitcast.44), kind=kOutput, calls=%fused_computation.3 | convolution fusion | flops 68353024 | bytes 8192 | tf_op jit(solution)/shard_map/dot_general | solution.py:245
  2.2 1.3 %bitcast_add_fusion.slot_ref = s32[1,1024]{1,0:T(1,128)} fusion(s32[1,1024]{1,0:T(1,128)S(1)} %bitcast.43, s32[1,1024,1]{1,2,0:T(1,128)} %param.13), kind=kLoop, calls=%fused_computation.48 | loop fusion | flops 2048 | bytes 12288 | tf_op jit(solution)/shard_map/add | solution.py:247
  3.4 0.1 fusion.7
  3.5 0.1 fusion.8
  3.6 0.1 fusion.9
  3.7 0.1 fusion.10
  3.8 0.1 fusion.11
  3.9 0.1 fusion.12
  4.1 0.7 concatenate.9.pick_ref
  4.7 1.0 slice_bitcast_fusion
  5.8 0.1 copy.13
  5.8 0.1 copy.11
  5.9 0.1 copy.10
  6.0 0.1 copy.9
  6.1 0.1 copy.8
  6.2 0.1 copy.12
  6.3 0.7 fusion.4.gather_ref
  7.0 0.2 broadcast_multiply_fusion
  7.2 0.1 mul.171
  7.3 0.1 copy.19
  7.4 0.1 mul.159
  7.5 0.1 copy.15
  7.6 0.1 mul.162
  7.8 0.1 copy.16
  7.9 0.1 mul.165
  8.0 0.1 copy.17
  8.1 0.1 mul.168
  8.2 0.1 copy.18
  8.4 0.1 mul.156
  8.5 0.1 copy.14
  8.6 0.8 concatenate.10.couple_ref
  9.4 77.5 %shard_map.73 = bf16[2048,256]{1,0:T(8,128)(2,1)} custom-call(f32[1024,256]{1,0:T(8,128)} %bitcast.40, f32[1024,256]{1,0:T(8,128)} %bitcast.41, f32[1024,256]{1,0:T(8,128)} %bitcast.42, s32[1,1024]{1,0:T(1,128)} %bitcast_add_fusion.slot_ref, bf16[384,256]{1,0:T(8,128)(2,1)} %concatenate.9.pick_ref, bf16[256,384]{1,0:T(8,128)(2,1)} %concatenate.10.couple_ref, ...), custom_call_target="tpu_custom_call" | custom-call | tf_op jit(solution)/shard_map/pallas_call | solution.py:257
  87.0 32.3 %all_to_all.5 = bf16[32,64,256]{2,1,0:T(8,128)(2,1)S(1)} all-to-all(bf16[32,64,256]{2,1,0:T(8,128)(2,1)} %bitcast.39), channel_id=1, replica_groups=mesh['gx'=4,'gy'=4,'gz'=2] {'gx','gy','gz'}, dimensions={0} | all-to-all | bytes 2097152 | tf_op jit(solution)/shard_map/all_to_all | solution.py:287
  119.3 1.5 %bitcast_convert_fusion = f32[2048,256]{1,0:T(8,128)} fusion(bf16[32,64,256]{2,1,0:T(8,128)(2,1)S(1)} %all_to_all.5), kind=kLoop, calls=%fused_computation.4 | loop fusion | flops 524288 | bytes 3145728 | tf_op jit(solution)/shard_map/convert_element_type | solution.py:294
  (13 shorter events, 0.1 us)

commit v2 on v1

v2 whole, which is shorter than its diff:
```python
import functools
import jax
import jax.numpy as jnp
import numpy as np
from jax import lax
from jax.experimental import pallas as pl
from jax.experimental.pallas import tpu as pltpu
from jax.sharding import PartitionSpec as P

COMP = 4
DOFS = 64
WIDTH = COMP * DOFS
STEPS = 2
LANES = 256
MESH = pl.DeviceIdType.MESH
BF = jnp.bfloat16
F32 = jnp.float32
NT = (((1,), (1,)), ((), ()))


def face_picks():
    local = np.arange(DOFS)
    coords = (local // 16, local // 4 % 4, local % 4)
    rests = (4 * coords[1] + coords[2], 4 * coords[0] + coords[2], 4 * coords[0] + coords[1])
    picks = []
    for direction in range(3):
        for level in (3, 0):
            match = (coords[direction] == level) & (rests[direction] == np.arange(16)[:, None])
            picks.append(np.kron(np.eye(COMP), match))
    return np.concatenate(picks, axis=0)


def kernel(
    dims, cap,
    state_ref, lower_ref, upper_ref, owner_ref, pick_ref, couple_ref,
    conv_hbm, inv_hbm, out_ref,
    conv_raw, inv_raw, conv_t, inv_t, state_t, lower_t, upper_t, work, rhs, vector,
    faces, landed, arriving, load_sem, send_sem, recv_sem,
):
    zones = state_ref.shape[0]
    blocks = zones // LANES
    axes = ("gx", "gy", "gz")
    counts = [lax.axis_size(a) for a in axes]
    place = [lax.axis_index(a) for a in axes]
    strides = (dims[1] * dims[2], dims[2], 1)

    def loads(block, inverse):
        part = pl.ds(block * LANES, LANES)
        if inverse:
            return pltpu.make_async_copy(inv_hbm.at[part], inv_raw.at[part], load_sem.at[blocks + block])
        return pltpu.make_async_copy(conv_hbm.at[part], conv_raw.at[part], load_sem.at[block])

    for block in range(blocks):
        loads(block, False).start()
    for block in range(blocks):
        loads(block, True).start()

    landed[...] = jnp.zeros_like(landed)
    barrier = pltpu.get_barrier_semaphore()
    ups = [place[d] < counts[d] - 1 for d in range(3)]
    downs = [place[d] > 0 for d in range(3)]
    for d in range(3):
        @pl.when(ups[d])
        def _(d=d):
            pl.semaphore_signal(barrier, 1, device_id={axes[d]: place[d] + 1}, device_id_type=MESH)

        @pl.when(downs[d])
        def _(d=d):
            pl.semaphore_signal(barrier, 1, device_id={axes[d]: place[d] - 1}, device_id_type=MESH)
    pl.semaphore_wait(barrier, sum(flag.astype(jnp.int32) for flag in ups + downs))

    for block in range(blocks):
        part = pl.ds(block * LANES, LANES)
        state_t[:, part] = state_ref[part, :].T
        lower_t[:, part] = lower_ref[part, :].T
        upper_t[:, part] = upper_ref[part, :].T

    rows = COMP * 16

    def exchange(step, d, side):
        row = pl.ds((2 * d + side) * rows, rows)
        if d == 0:
            near = zones - strides[0] if side == 0 else 0
            lane = pl.ds(near, strides[0])
        else:
            lane = pl.ds(0, zones)
        return pltpu.make_async_remote_copy(
            src_ref=faces.at[step, row, lane],
            dst_ref=landed.at[step, row, lane],
            send_sem=send_sem.at[step, 2 * d + side],
            recv_sem=recv_sem.at[step, 2 * d + side],
            device_id={axes[d]: place[d] + 1 if side == 0 else place[d] - 1},
            device_id_type=MESH,
        )

    level8 = lax.broadcasted_iota(jnp.int32, (8, 128), 0)

    def merged(a, b, stride):
        odd = level8 // stride % 2 == 1
        return jnp.where(odd, b, a) + pltpu.roll(jnp.where(odd, a, b), 8 - stride, 0)

    def turn(raw, target, lane, chunk):
        col = pl.ds(pl.multiple_of(chunk * 128, 128), 128)
        value = raw[lane, col].T

        def store():
            target[col, lane] = value

        return store

    groups = DOFS // 8

    def apply(matrix, block, raw, finish):
        halves = [pl.ds(block * LANES + half * 128, 128) for half in range(LANES // 128)]
        if raw is not None:
            for lane in halves:
                for pair in range(4):
                    turn(raw, matrix, lane, pair)()

        @pl.loop(0, groups)
        def _(group):
            for lane in halves:
                stack = [[] for _ in range(COMP)]
                for pair in range(4):
                    store = None
                    if raw is not None:
                        store = turn(raw, matrix, lane, jnp.minimum(group + 1, groups - 1) * 4 + pair)
                    base = pl.multiple_of(group * 512 + pair * 128, 128)
                    m = [
                        [matrix[pl.ds(base + 64 * i + 16 * b, 16), lane].astype(F32) for b in range(4)]
                        for i in range(2)
                    ]
                    for c in range(COMP):
                        sums = [None, None]
                        for b in range(4):
                            row = c * DOFS + 16 * b
                            v = vector[row : row + 16, lane]
                            for i in range(2):
                                term = m[i][b] * v
                                sums[i] = term if b == 0 else sums[i] + term
                        node = merged(*[total[:8] + total[8:] for total in sums], 1)
                        stride = 2
                        while len(stack[c]) and stack[c][-1][0] == stride:
                            node = merged(stack[c].pop()[1], node, stride)
                            stride *= 2
                        stack[c].append((stride, node))
                    if store is not None:
                        store()
                for c in range(COMP):
                    row = pl.ds(pl.multiple_of(c * DOFS + group * 8, 8), 8)
                    finish(row, lane, stack[c][0][1])

    lane_id = lax.broadcasted_iota(jnp.int32, (rows, zones), 1)

    def keep(row, lane, value):
        rhs[row, lane] = value

    def advance(row, lane, value):
        moved = state_t[row, lane] + value
        state_t[row, lane] = jnp.minimum(jnp.maximum(moved, lower_t[row, lane]), upper_t[row, lane])

    for step in range(STEPS):
        work[...] = state_t[...].astype(BF)
        vector[...] = work[...].astype(F32)
        faces[step] = jnp.dot(pick_ref[...], work[...], preferred_element_type=F32).astype(BF)
        for d in range(3):
            @pl.when(ups[d])
            def _(d=d):
                exchange(step, d, 0).start()

            @pl.when(downs[d])
            def _(d=d):
                exchange(step, d, 1).start()
        for block in range(blocks):
            if step == 0:
                loads(block, False).wait()
            apply(conv_t, block, conv_raw if step == 0 else None, keep)
        for d in range(3):
            @pl.when(downs[d])
            def _(d=d):
                exchange(step, d, 0).wait_recv()

            @pl.when(ups[d])
            def _(d=d):
                exchange(step, d, 1).wait_recv()
        for d in range(3):
            s = strides[d]
            n = dims[d]
            index = lane_id // s % n
            far = (n - 1) * s
            for side in range(2):
                row = pl.ds((2 * d + side) * rows, rows)
                mine = faces[step, row, :].astype(F32)
                other = landed[step, row, :].astype(F32)
                if side == 0:
                    inner = pltpu.roll(mine, s, 1)
                    outer = pltpu.roll(other, zones - far, 1)
                    value = jnp.where(index == 0, outer, inner)
                else:
                    inner = pltpu.roll(mine, zones - s, 1)
                    outer = pltpu.roll(other, far, 1)
                    value = jnp.where(index == n - 1, outer, inner)
                value = value.astype(BF)
                for c in range(COMP):
                    face = 2 * d + side
                    arriving[c, face * 16 : face * 16 + 16, :] = value[c * 16 : c * 16 + 16]
        for c in range(COMP):
            row = slice(c * DOFS, (c + 1) * DOFS)
            flux = jnp.dot(couple_ref[...], arriving[c], preferred_element_type=F32)
            vector[row, :] = (rhs[row, :] + flux).astype(BF).astype(F32)
        for block in range(blocks):
            if step == 0:
                loads(block, True).wait()
            apply(inv_t, block, inv_raw if step == 0 else None, advance)
        for d in range(3):
            @pl.when(ups[d])
            def _(d=d):
                exchange(step, d, 0).wait_send()

            @pl.when(downs[d])
            def _(d=d):
                exchange(step, d, 1).wait_send()

    work[...] = state_t[...].astype(BF)
    owner = owner_ref[...]
    devices = out_ref.shape[0] // cap
    named = lax.broadcasted_iota(jnp.int32, (devices, zones), 0) == owner
    earlier = lax.broadcasted_iota(jnp.int32, (zones, zones), 0) < lax.broadcasted_iota(
        jnp.int32, (zones, zones), 1
    )
    before = jnp.dot(
        jnp.where(named, 1.0, 0.0).astype(BF),
        jnp.where(earlier, 1.0, 0.0).astype(BF),
        preferred_element_type=F32,
    )
    rank = jnp.sum(jnp.where(named, before, 0.0), axis=0, keepdims=True).astype(jnp.int32)
    slots = jnp.broadcast_to(owner * cap + rank, (LANES, zones))
    level = lax.broadcasted_iota(jnp.int32, (LANES, zones), 0)

    @pl.loop(0, out_ref.shape[0] // LANES)
    def _(group):
        start = pl.multiple_of(group * LANES, LANES)
        onehot = jnp.where(slots == level + start, 1.0, 0.0).astype(BF)
        out_ref[pl.ds(start, LANES), :] = lax.dot_general(
            onehot, work[...], NT, preferred_element_type=F32
        ).astype(BF)


def shards(state, convection, inverse_mass, face_coupling, lower_bound, upper_bound, new_owner):
    ex, ey, ez, width = state.shape
    zones = ex * ey * ez
    devices = lax.axis_size(("gx", "gy", "gz"))
    capacity = max(2, 2 * zones // devices)
    pick = jnp.asarray(face_picks(), BF)
    total = devices * capacity
    vmem = pl.BlockSpec(memory_space=pltpu.VMEM)
    hbm = pl.BlockSpec(memory_space=pl.ANY)
    blocks = zones // LANES
    entries = DOFS * DOFS
    outgoing = pl.pallas_call(
        functools.partial(kernel, (ex, ey, ez), capacity),
        out_shape=jax.ShapeDtypeStruct((total, width), BF),
        in_specs=[vmem] * 6 + [hbm] * 2,
        out_specs=vmem,
        scratch_shapes=[
            pltpu.VMEM((zones, entries), BF),
            pltpu.VMEM((zones, entries), BF),
            pltpu.VMEM((entries, zones), BF),
            pltpu.VMEM((entries, zones), BF),
            pltpu.VMEM((width, zones), F32),
            pltpu.VMEM((width, zones), F32),
            pltpu.VMEM((width, zones), F32),
            pltpu.VMEM((width, zones), BF),
            pltpu.VMEM((width, zones), F32),
            pltpu.VMEM((width, zones), F32),
            pltpu.VMEM((STEPS, 6 * COMP * 16, zones), BF),
            pltpu.VMEM((STEPS, 6 * COMP * 16, zones), BF),
            pltpu.VMEM((COMP, 96, zones), BF),
            pltpu.SemaphoreType.DMA((2 * blocks,)),
            pltpu.SemaphoreType.DMA((STEPS, 6)),
            pltpu.SemaphoreType.DMA((STEPS, 6)),
        ],
        compiler_params=pltpu.CompilerParams(
            collective_id=0, has_side_effects=True, vmem_limit_bytes=60 * 1024 * 1024
        ),
    )(
        state.reshape(zones, width), lower_bound.reshape(zones, width),
        upper_bound.reshape(zones, width), new_owner.reshape(1, zones), pick, face_coupling.T,
        convection.reshape(zones, entries), inverse_mass.reshape(zones, entries),
    )
    arrived = lax.all_to_all(
        outgoing.reshape(devices, capacity, width),
        ("gx", "gy", "gz"),
        split_axis=0,
        concat_axis=0,
        tiled=True,
    )
    return arrived.reshape(total, width).astype(F32)


def solution(mesh):
    in_specs = (
        P("gx", "gy", "gz", None),
        P("gx", "gy", "gz", None),
        P("gx", "gy", "gz", None),
        P(),
        P("gx", "gy", "gz", None),
        P("gx", "gy", "gz", None),
        P(("gx", "gy", "gz"), None, None),
    )
    out_specs = P(("gx", "gy", "gz"), None)
    return jax.shard_map(shards, mesh=mesh, in_specs=in_specs, out_specs=out_specs, check_vma=False)
```

time: 121 us -> 82 us (0.68)
  Pallas kernels: 77.5 us -> 47.9 us
  other arithmetic: 5.81 us -> 1.55 us
  local copies, waits for them, and re-layouts: 3.74 us -> 0 us
  matrix products: 1.3 us -> 0 us
    pallas_call x1, Pallas kernels: 77.5 us -> 47.9 us  [shards(): pl.pallas_call(functools.partial(kernel, (ex, ey, ez), capacity), out_sha...]
    transpose x7 -> x0, local copies, waits for them, and re-layouts: 1.51 us -> none  [face_tables(): block.T[None, :, None, :]]
    mul x12 -> x0, local copies, waits for them, and re-layouts: 1.38 us -> none  [face_tables(): identity[:, None, :, None] * block.T[None, :, None, :]]
    convert_element_type x3 -> x0, other arithmetic: 1.38 us -> none  [the longest x1 0.7 us: shards(): gather = (jnp.arange(DOFS)[:, None] == (jnp.arange(DOFS * 16) // 16)[None...]
    add x3 -> x0, other arithmetic: 1.31 us -> none  [the longest x1 1.29 us: shards(): slot = (owner * capacity + rank).reshape(1, zones)]
    dot_general x1 -> x0, matrix products: 1.3 us -> none  [shards(): running = jnp.dot(lower_tri, onehot, preferred_element_type=F32)]
where the time goes in v2:
time: 82 us; the launch traced here: 81.8 us
  Pallas kernels  47.9 us (58%)
  blocking collectives  32.3 us (39%)
  other arithmetic  1.55 us (2%)
    pallas_call x1, Pallas kernels, shards(): pl.pallas_call(functools.partial(kernel, (ex, ey, ez), capacity), out_sha...  47.9 us
    all_to_all x1, blocking collectives, shards(): lax.all_to_all(outgoing.reshape(devices, capacity, width), ('gx', 'gy', '...  32.3 us

profile of v2, /device:TPU:0, one launch (start us, length us, event | category | flops | bytes accessed | tf_op | source)
XLA Modules:
  0.0 81.8 jit_solution(14020495903542264745)
XLA Ops:
  0.0 47.9 %shard_map.82 = bf16[2048,256]{1,0:T(8,128)(2,1)} custom-call(f32[1024,256]{1,0:T(8,128)} %bitcast.14, f32[1024,256]{1,0:T(8,128)} %bitcast.15, f32[1024,256]{1,0:T(8,128)} %bitcast.16, s32[1,1024]{1,0:T(1,128)} %bitcast.18, bf16[384,256]{1,0:T(8,128)(2,1)} %constant.2.clone.pick_ref, bf16[64,96]{1,0:T(8,128)(2,1)} %bitcast.17, bf16[1024,4096]{1,0:T(8,128)(2,1)} %bitcast.11, ...), custom_call_target="tpu_custom_call" | custom-call | tf_op jit(solution)/shard_map/pallas_call | solution.py:260
  47.9 32.3 %all_to_all.5 = bf16[32,64,256]{2,1,0:T(8,128)(2,1)S(1)} all-to-all(bf16[32,64,256]{2,1,0:T(8,128)(2,1)} %bitcast.13), channel_id=1, replica_groups=mesh['gx'=4,'gy'=4,'gz'=2] {'gx','gy','gz'}, dimensions={0} | all-to-all | bytes 2097152 | tf_op jit(solution)/shard_map/all_to_all | solution.py:291
  80.2 1.5 %bitcast_convert_fusion = f32[2048,256]{1,0:T(8,128)} fusion(bf16[32,64,256]{2,1,0:T(8,128)(2,1)S(1)} %all_to_all.5), kind=kLoop, calls=%fused_computation | loop fusion | flops 524288 | bytes 3145728 | tf_op jit(solution)/shard_map/convert_element_type | solution.py:298
